TPU v7x, 32 devices: a whole 2x2x4 slice. The times are simulated.
32 devices in a mesh: lon: 8 (over z, core), lat: 4 (over y, x).
Axes of the slice: x: 2, y: 2, z: 4, core: 2. Of those that a mesh axis runs over, the one named last changes fastest.
Arguments:
- fine_input: bfloat16 [4, 48, 192, 384], P(None, 'lat', 'lon'), may hold values from -10 to 10
- merge_gain: float32 [1536], replicated, may hold values from 0.5 to 1.5
- merge_bias: float32 [1536], replicated, may hold values from -1.5 to 1.5
- merge_weight: bfloat16 [1536, 768], P('lat'), may hold values from -2 to 2
- coarse_gain: float32 [768], replicated, may hold values from 0.5 to 1.5
- coarse_bias: float32 [768], replicated, may hold values from -1.5 to 1.5
- coarse_qkv: bfloat16 [768, 2304], P('lat'), may hold values from -2 to 2
- coarse_out: bfloat16 [768, 768], P('lat'), may hold values from -0.21875 to 0.21875
Outputs:
- coarse_output: bfloat16 [4, 24, 96, 768], P(None, 'lat', 'lon')
All inputs are finite; a program needn't handle non-finite values.
Results may differ from a plain program's by a relative error of at most 0.013.
Values may be sent and summed in bfloat16 or wider, within the bound.
A program may use at most 128 MiB of HBM per device.

v0:
```python
import jax
import jax.numpy as jnp
from jax import lax
from jax.sharding import PartitionSpec as P

HEADS2 = 24


EPSILON = 1e-05


def passed_along(value, axis, steps):
    count = lax.axis_size(axis)
    pairs = [(source, (source + steps) % count) for source in range(count)]
    return lax.ppermute(value, axis, pairs)


def normalize(values, norm_gain, norm_bias):
    average = jnp.mean(values, axis=-1, keepdims=True)
    centered = values - average
    spread = jnp.mean(centered * centered, axis=-1, keepdims=True)
    return centered * lax.rsqrt(spread + EPSILON) * norm_gain + norm_bias


def group_ids(level_count, row_start, row_count, row_total):
    level_index = (jnp.arange(level_count, dtype=jnp.int32) + 1) % level_count
    row_index = (row_start + jnp.arange(row_count, dtype=jnp.int32) + 3) % row_total
    level_group = jnp.floor_divide(level_index - 1, 2)
    row_group = jnp.floor_divide(row_index - 3, 6)
    return level_group[:, None] * 65536 + row_group[None, :]


def attend(framed, group_grid, qkv_weight, head_count):
    level_count, row_count, col_count, width = framed.shape
    head_depth = width // head_count
    flat_rows = framed.reshape(-1, width)
    projected = jnp.dot(flat_rows, qkv_weight, preferred_element_type=jnp.float32).astype(
        jnp.bfloat16
    )
    window_shape = (level_count // 2, 2, row_count // 6, 6, col_count // 12, 12)
    windows = projected.reshape(window_shape + (3, head_count, head_depth))
    windows = windows.transpose(0, 2, 4, 1, 3, 5, 6, 7, 8).reshape(
        -1, 144, 3, head_count, head_depth
    )
    key_grid = jnp.broadcast_to(group_grid[:, :, None], (level_count, row_count, col_count))
    key_windows = key_grid.reshape(window_shape).transpose(0, 2, 4, 1, 3, 5).reshape(-1, 144)
    allowed = key_windows[:, :, None] == key_windows[:, None, :]
    scores = jnp.einsum(
        "wqhd,wkhd->whqk", windows[:, :, 0], windows[:, :, 1], preferred_element_type=jnp.float32
    ) * head_depth ** (-0.5)
    scores = jnp.where(allowed[:, None], scores, -jnp.inf)
    row_peak = jnp.max(scores, axis=-1, keepdims=True)
    weights = jnp.exp(scores - row_peak)
    probabilities = (weights / jnp.sum(weights, axis=-1, keepdims=True)).astype(jnp.bfloat16)
    context = jnp.einsum(
        "whqk,wkhd->wqhd", probabilities, windows[:, :, 2], preferred_element_type=jnp.float32
    ).astype(jnp.bfloat16)
    context = context.reshape(level_count // 2, row_count // 6, col_count // 12, 2, 6, 12, width)
    return context.transpose(0, 3, 1, 4, 2, 5, 6).reshape(level_count, row_count, col_count, width)


def attend_pairs(framed, group_grid, qkv_weight, head_count):
    level_count, row_count, col_count, width = framed.shape
    level_pairs = framed.reshape(level_count // 2, 2, row_count, col_count, width)
    pair_ids = group_grid.reshape(level_count // 2, 2, row_count)

    def one_pair(pair_items):
        return attend(pair_items[0], pair_items[1], qkv_weight, head_count)

    context = lax.map(one_pair, (level_pairs, pair_ids))
    return context.reshape(level_count, row_count, col_count, width)


def rolled_context(normed, qkv_weight, head_count):
    level_count, row_count, col_count, width = normed.shape
    rim_rows = passed_along(normed[:, :3], "lat", -1)
    framed = jnp.concatenate([normed[:, 3:], rim_rows], axis=1)
    rim_cols = passed_along(framed[:, :, :6], "lon", -1)
    framed = jnp.concatenate([framed[:, :, 6:], rim_cols], axis=2)
    framed = jnp.roll(framed, -1, axis=0)
    grid_ids = group_ids(
        level_count, lax.axis_index("lat") * row_count, row_count, row_count * lax.axis_size("lat")
    )
    context = jnp.roll(attend_pairs(framed, grid_ids, qkv_weight, head_count), 1, axis=0)
    back_cols = passed_along(context[:, :, col_count - 6 :], "lon", 1)
    context = jnp.concatenate([back_cols, context[:, :, : col_count - 6]], axis=2)
    back_rows = passed_along(context[:, row_count - 3 :], "lat", 1)
    return jnp.concatenate([back_rows, context[:, : row_count - 3]], axis=1)


def sublayer(inputs, norm_gain, norm_bias, fetch_weight, position, head_count):
    width = inputs.shape[3]
    normed = normalize(inputs.astype(jnp.float32), norm_gain, norm_bias).astype(jnp.bfloat16)
    qkv_weight = fetch_weight(position)
    context = rolled_context(normed, qkv_weight, head_count)
    out_weight = fetch_weight(position + 1)
    branch = jnp.dot(context.reshape(-1, width), out_weight, preferred_element_type=jnp.float32)
    return (inputs.astype(jnp.float32) + branch.reshape(inputs.shape)).astype(jnp.bfloat16)


def merge_patches(fine, norm_gain, norm_bias, weight):
    level_count, row_count, col_count, width = fine.shape
    patches = fine.reshape(level_count, row_count // 2, 2, col_count // 2, 2, width)
    patches = patches.transpose(0, 1, 3, 2, 4, 5).reshape(
        level_count, row_count // 2, col_count // 2, 4 * width
    )
    normed = normalize(patches.astype(jnp.float32), norm_gain, norm_bias).astype(jnp.bfloat16)
    merged = jnp.dot(normed.reshape(-1, 4 * width), weight, preferred_element_type=jnp.float32)
    return merged.astype(jnp.bfloat16).reshape(
        level_count, row_count // 2, col_count // 2, weight.shape[1]
    )


def shards(
    fine_input,
    merge_gain,
    merge_bias,
    merge_weight,
    coarse_gain,
    coarse_bias,
    coarse_qkv,
    coarse_out,
):
    raw_weights = (merge_weight, coarse_qkv, coarse_out)

    def fetch_weight(position):
        return lax.all_gather(raw_weights[position], "lat", axis=0, tiled=True)

    coarse_input = merge_patches(fine_input, merge_gain, merge_bias, fetch_weight(0))
    return sublayer(coarse_input, coarse_gain, coarse_bias, fetch_weight, 1, HEADS2)


def solution(mesh):
    in_specs = (
        P(None, "lat", "lon", None),
        P(),
        P(),
        P("lat", None),
        P(),
        P(),
        P("lat", None),
        P("lat", None),
    )
    out_specs = P(None, "lat", "lon", None)
    return jax.shard_map(shards, mesh=mesh, in_specs=in_specs, out_specs=out_specs, check_vma=False)
```

profile of v0, /device:TPU:0, one launch (start us, length us, event | category | flops | bytes accessed | tf_op | source)
XLA Modules:
  0.0 151.0 jit_solution(5906005166033488279)
XLA Ops:
  10.4 1.8 %multiply_reduce_fusion = f32[4,6,12]{2,1,0:T(8,128)S(1)} fusion(f32[4,6,12]{2,1,0:T(8,128)S(1)} %broadcast_multiply_fusion, f32[4,6,2,12,2,384]{5,4,3,2,1,0:T(2,128)S(1)} %reshape.243), kind=kLoop, calls=%fused_computation.24 | loop fusion | flops 1326816 | bytes 1771776 | tf_op jit(solution)/shard_map/reduce_sum | solution.py:21
  13.6 2.6 %reshape.240 = f32[288,1536]{1,0:T(8,128)} reshape(f32[4,6,12,2,2,384]{5,4,3,2,1,0:T(2,128)S(1)} %bitcast.55) | data formatting | bytes 3538944 | tf_op jit(solution)/shard_map/convert_element_type | solution.py:107
  16.2 33.1 %all-gather.4.cloned.1.call-done = bf16[1536,768]{1,0:T(8,128)(2,1)} async-done(((bf16[384,768]{1,0:T(8,128)(2,1)}), bf16[1536,768]{1,0:T(8,128)(2,1)}) %all-gather.4.cloned.1.call-update) | async-done | bytes 2359312 | tf_op jit(solution)/shard_map/all_gather | solution.py:127
  49.3 3.2 %fusion.35 = (f32[288]{0:T(512)S(1)}, f32[288,768]{1,0:T(8,128)S(1)}) fusion(bf16[1536,768]{1,0:T(8,128)(2,1)} %all-gather.4.cloned.1.call-done, f32[288,1536]{1,0:T(8,128)} %reshape.240, f32[1536]{0:T(1024)S(1)} %copy-done.8, f32[1536]{0:T(1024)S(1)} %copy-done.9, f32[288]{0:T(512)S(1)} %rsqrt.23, f32[288]{0:T(512)S(1)} %copy-done.7), kind=kOutput, calls=%fused_computation.76 | convolution fusion | flops 682352384 | bytes 5029248 | tf_op jit(solution)/shard_map/dot_general | solution.py:108
  53.7 1.5 collective-permute-start
  55.2 9.3 %collective-permute-done = bf16[4,3,12,768]{3,2,1,0:T(8,128)(2,1)S(1)} collective-permute-done((bf16[4,3,12,768]{3,2,1,0:T(8,128)(2,1)S(1)}, bf16[4,3,12,768]{3,2,1,0:T(8,128)(2,1)S(1)}, u32[]{:S(2)}, u32[]{:S(2)}) %collective-permute-start) | collective-permute-done | bytes 221216 | tf_op jit(solution)/shard_map/ppermute | solution.py:15
  64.7 4.2 %collective-permute-done.1 = bf16[4,6,6,768]{3,2,1,0:T(8,128)(2,1)S(1)} collective-permute-done((bf16[4,6,6,768]{3,2,1,0:T(8,128)(2,1)S(1)}, bf16[4,6,6,768]{3,2,1,0:T(8,128)(2,1)S(1)}, u32[]{:S(2)}, u32[]{:S(2)}) %collective-permute-start.1) | collective-permute-done | bytes 221216 | tf_op jit(solution)/shard_map/ppermute | solution.py:15
  70.0 29.7 %all-gather.6.cloned.1.call-done = bf16[768,2304]{1,0:T(8,128)(2,1)} async-done(((bf16[192,2304]{1,0:T(8,128)(2,1)}), bf16[768,2304]{1,0:T(8,128)(2,1)}) %all-gather.6.cloned.1.call-update) | async-done | bytes 3538960 | tf_op jit(solution)/shard_map/all_gather | solution.py:127
  99.7 23.7 %while.10 = (s32[]{:T(128)}, bf16[2,2,6,12,768]{4,3,2,1,0:T(8,128)(2,1)}, bf16[2,2,6,12,768]{4,3,2,1,0:T(8,128)(2,1)}, bf16[768,2304]{1,0:T(8,128)(2,1)}, s32[2,2,6]{2,1,0:T(2,128)S(1)}, /*index=5*/s32[]{:T(128)}) while((s32[]{:T(128)}, bf16[2,2,6,12,768]{4,3,2,1,0:T(8,128)(2,1)}, bf16[2,2,6,12,768]{4,3,2,1,0:T(8,128)(2,1)}, ...), condition=%wide.region_7.8_spmd, body=%wide.region_4.7_spmd.sunk | while | flops 577753472 | bytes 21084184 | solution.py:70
  100.7 2.7 %convolution_convert_fusion.3 = bf16[144,2304]{1,0:T(8,128)(2,1)S(1)} fusion(bf16[144,768]{1,0:T(8,128)(2,1)S(1)} %reshape.246, bf16[768,2304]{1,0:T(8,128)(2,1)} %get-tuple-element.103), kind=kOutput, calls=%fused_computation.1.clone.1 | convolution fusion | flops 509939712 | bytes 4423680 | tf_op jit(solution)/shard_map/while/body/eval_jaxpr/dot_general | solution.py:37
  103.5 1.4 copy.30
  104.9 1.8 %fusion.46 = f32[24,144,144]{1,2,0:T(8,128)S(1)} fusion(bf16[1,144,3,24,32]{1,4,3,2,0:T(8,128)(2,1)} %bitcast.53), kind=kOutput, calls=%fused_computation.13.clone.1 | convolution fusion | flops 31850496 | bytes 2777088 | tf_op jit(solution)/shard_map/while/body/eval_jaxpr/wqhd,wkhd->whqk/dot_general | solution.py:48
  106.9 1.1 fusion.47
  108.0 1.5 fusion.48
  112.6 2.7 %convolution_convert_fusion.3 = bf16[144,2304]{1,0:T(8,128)(2,1)S(1)} fusion(bf16[144,768]{1,0:T(8,128)(2,1)S(1)} %reshape.246, bf16[768,2304]{1,0:T(8,128)(2,1)} %get-tuple-element.103), kind=kOutput, calls=%fused_computation.1.clone.1 | convolution fusion | flops 509939712 | bytes 4423680 | tf_op jit(solution)/shard_map/while/body/eval_jaxpr/dot_general | solution.py:37
  115.3 1.4 copy.30
  116.7 1.8 %fusion.46 = f32[24,144,144]{1,2,0:T(8,128)S(1)} fusion(bf16[1,144,3,24,32]{1,4,3,2,0:T(8,128)(2,1)} %bitcast.53), kind=kOutput, calls=%fused_computation.13.clone.1 | convolution fusion | flops 31850496 | bytes 2777088 | tf_op jit(solution)/shard_map/while/body/eval_jaxpr/wqhd,wkhd->whqk/dot_general | solution.py:48
  118.8 1.1 fusion.47
  119.9 1.6 %fusion.48 = bf16[1,144,24,32]{1,3,2,0:T(8,128)(2,1)S(1)} fusion(f32[24,144,144]{1,2,0:T(8,128)S(1)} %get-tuple-element.86, f32[24,144]{1,0:T(8,128)S(1)} %get-tuple-element.87, bf16[1,144,3,24,32]{1,4,3,2,0:T(8,128)(2,1)} %bitcast.54), kind=kOutput, calls=%fused_computation.11.clone.1 | convolution fusion | flops 32956416 | bytes 2618880 | tf_op jit(solution)/shard_map/while/body/eval_jaxpr/whqk,wkhd->wqhd/dot_general | solution.py:55
  125.6 7.9 %collective-permute-done.2 = bf16[4,6,6,768]{3,2,1,0:T(8,128)(2,1)S(1)} collective-permute-done((bf16[4,6,6,768]{3,2,1,0:T(8,128)(2,1)S(1)}, bf16[4,6,6,768]{3,2,1,0:T(8,128)(2,1)S(1)}, u32[]{:S(2)}, u32[]{:S(2)}) %collective-permute-start.2) | collective-permute-done | bytes 221216 | tf_op jit(solution)/shard_map/ppermute | solution.py:15
  133.8 1.4 collective-permute-start.3
  135.3 6.2 %collective-permute-done.3 = bf16[4,3,12,768]{3,2,1,0:T(8,128)(2,1)S(1)} collective-permute-done((bf16[4,3,12,768]{3,2,1,0:T(8,128)(2,1)S(1)}, bf16[4,3,12,768]{3,2,1,0:T(8,128)(2,1)S(1)}, u32[]{:S(2)}, u32[]{:S(2)}) %collective-permute-start.3) | collective-permute-done | bytes 221216 | tf_op jit(solution)/shard_map/ppermute | solution.py:15
  141.5 1.9 %fusion.11 = bf16[4,6,12,768]{3,2,1,0:T(8,128)(2,1)S(1)} fusion(f32[4,6,12,768]{3,2,1,0:T(8,128)S(1)} %copy-done.1, bf16[768,768]{1,0:T(8,128)(2,1)} %all-gather.8.cloned.1.call-done, bf16[4,3,12,768]{3,2,1,0:T(8,128)(2,1)S(1)} %get-tuple-element.46, bf16[4,3,12,768]{3,2,1,0:T(8,128)(2,1)S(1)} %collective-permute-done.3), kind=kOutput, calls=%fused_computation.26 | convolution fusion | flops 340402176 | bytes 2949120 | tf_op jit(solution)/shard_map/dot_general | solution.py:97
  143.4 1.1 copy.19
  (78 shorter events, 16.5 us)
Async XLA Ops:
  6.5 2.2 %copy-start.2 = (bf16[4,12,24,384]{3,2,1,0:T(8,128)(2,1)S(1)}, bf16[4,12,24,384]{3,2,1,0:T(8,128)(2,1)}, u32[]{:S(2)}) copy-start(bf16[4,12,24,384]{3,2,1,0:T(8,128)(2,1)} %param.10) | copy-start | bytes 2654212
  6.5 42.7 %all-gather.4.cloned.1.call-start = ((), (), s32[]{:S(2)}) async-start(), calls=%async_computation | async-start | bytes 2949120 | tf_op jit(solution)/shard_map/all_gather | solution.py:127
  7.3 92.4 %all-gather.6.cloned.1.call-start = ((), (), s32[]{:S(2)}) async-start(), calls=%async_computation.1 | async-start | bytes 4423680 | tf_op jit(solution)/shard_map/all_gather | solution.py:127
  8.0 127.2 %all-gather.8.cloned.1.call-start = ((), (), s32[]{:S(2)}) async-start(), calls=%async_computation.2 | async-start | bytes 1474560 | tf_op jit(solution)/shard_map/all_gather | solution.py:127
  13.5 35.7 %copy-start.7 = (f32[288]{0:T(512)S(1)}, f32[288]{0:T(512)}, u32[]{:S(2)}) copy-start(f32[288]{0:T(512)} %div.46) | copy-start | bytes 3460
  13.5 35.7 %copy-start.8 = (f32[1536]{0:T(1024)S(1)}, f32[1536]{0:T(1024)}, u32[]{:S(2)}) copy-start(f32[1536]{0:T(1024)} %param.12) | copy-start | bytes 18436
  13.6 35.7 %copy-start.9 = (f32[1536]{0:T(1024)S(1)}, f32[1536]{0:T(1024)}, u32[]{:S(2)}) copy-start(f32[1536]{0:T(1024)} %param.11) | copy-start | bytes 18436
  52.5 0.7 copy-start.5
  52.5 0.7 copy-start.6
  52.7 1.0 copy-start
  53.7 10.8 %collective-permute-start = (bf16[4,3,12,768]{3,2,1,0:T(8,128)(2,1)S(1)}, bf16[4,3,12,768]{3,2,1,0:T(8,128)(2,1)S(1)}, u32[]{:S(2)}, u32[]{:S(2)}) collective-permute-start(bf16[4,3,12,768]{3,2,1,0:T(8,128)(2,1)S(1)} %get-tuple-element.50), channel_id=1, source_target_pairs={{0,3},{1,0},{2,1},{3,2},{4,7},{5,4},{6,5},{7,6},{8,11},{9,8},{10,9... | collective-permute-start | bytes 663560 | tf_op jit(solution)/shard_map/ppermute | solution.py:15
  64.6 4.3 %collective-permute-start.1 = (bf16[4,6,6,768]{3,2,1,0:T(8,128)(2,1)S(1)}, bf16[4,6,6,768]{3,2,1,0:T(8,128)(2,1)S(1)}, u32[]{:S(2)}, u32[]{:S(2)}) collective-permute-start(bf16[4,6,6,768]{3,2,1,0:T(8,128)(2,1)S(1)} %get-tuple-element.48), channel_id=1, source_target_pairs={{0,28},{4,0},{8,4},{12,8},{16,12},{20,16},{24,20},{28,24},{1,29},{... | collective-permute-start | bytes 663560 | tf_op jit(solution)/shard_map/ppermute | solution.py:15
  109.5 1.1 copy-start.3
  110.7 0.9 copy-start.4
  121.4 1.1 copy-start.3
  122.6 0.9 copy-start.4
  125.4 16.1 %copy-start.1 = (f32[4,6,12,768]{3,2,1,0:T(8,128)S(1)}, f32[4,6,12,768]{3,2,1,0:T(8,128)}, u32[]{:S(2)}) copy-start(f32[4,6,12,768]{3,2,1,0:T(8,128)} %copy-done) | copy-start | bytes 2654212
  125.5 8.0 %collective-permute-start.2 = (bf16[4,6,6,768]{3,2,1,0:T(8,128)(2,1)S(1)}, bf16[4,6,6,768]{3,2,1,0:T(8,128)(2,1)S(1)}, u32[]{:S(2)}, u32[]{:S(2)}) collective-permute-start(bf16[4,6,6,768]{3,2,1,0:T(8,128)(2,1)S(1)} %fusion.24), channel_id=1, source_target_pairs={{0,4},{4,8},{8,12},{12,16},{16,20},{20,24},{24,28},{28,0},{1,5},{5... | collective-permute-start | bytes 663560 | tf_op jit(solution)/shard_map/ppermute | solution.py:15
  133.8 7.7 %collective-permute-start.3 = (bf16[4,3,12,768]{3,2,1,0:T(8,128)(2,1)S(1)}, bf16[4,3,12,768]{3,2,1,0:T(8,128)(2,1)S(1)}, u32[]{:S(2)}, u32[]{:S(2)}) collective-permute-start(bf16[4,3,12,768]{3,2,1,0:T(8,128)(2,1)S(1)} %get-tuple-element.45), channel_id=1, source_target_pairs={{0,1},{1,2},{2,3},{3,0},{4,5},{5,6},{6,7},{7,4},{8,9},{9,10},{10,1... | collective-permute-start | bytes 663560 | tf_op jit(solution)/shard_map/ppermute | solution.py:15
Sparse Core Ops, SparseCore 0:
  9.2 40.0 all-gather.3
  51.1 48.5 all-gather.5
  101.5 27.5 all-gather.7
where the time goes:
time: 152 us; the launch traced here: 151 us
  waiting for transfers between devices  92.5 us (61%)
  local copies, waits for them, and re-layouts  17.8 us (12%)
  matrix products  17.1 us (11%)
  between operations  13.3 us (9%)
  other arithmetic  7.01 us (5%)
  starting transfers between devices  3.1 us (2%)
    all_gather x3, waiting for transfers between devices, fetch_weight(): return lax.all_gather(raw_weights[position], 'lat', axis=0, tiled=True)  62.8 us
    ppermute x4, waiting for transfers between devices, passed_along(): return lax.ppermute(value, axis, pairs)  27.6 us
    dot_general x2, matrix products, attend(): jnp.dot(flat_rows, qkv_weight, preferred_element_type=jnp.float32)  5.39 us
    convert_element_type x3, local copies, waits for them, and re-layouts, merge_patches(): patches.astype(jnp.float32)  4.11 us
    dot_general x2, matrix products, attend(): jnp.einsum('wqhd,wkhd->whqk', windows[:, :, 0], windows[:, :, 1], preferr...  3.57 us
    dot_general x1, matrix products, merge_patches(): jnp.dot(normed.reshape(-1, 4 * width), weight, preferred_element_type=jnp...  3.25 us
  transfers between devices with their start and end apart: 7, of which 6 were waited for; matrix products, arithmetic and copies ran while one was open for 24% of the time, Pallas kernels for 0%

commit v1 on v0

v1 whole, which is shorter than its diff:
```python
import functools

import jax
import jax.numpy as jnp
import numpy as np
from jax import lax
from jax.experimental import pallas as pl
from jax.experimental.pallas import tpu as pltpu
from jax.sharding import PartitionSpec as P

HEADS2 = 24
EPSILON = 1e-05
MESH = pl.DeviceIdType.MESH
BLOCKED = -1e30
SLOTS = 4
PARTS = 6


def swapped(index, bits):
    bit = 1
    while bit <= bits:
        if bits & bit:
            index = index + bit - 2 * bit * ((index // bit) % 2)
        bit *= 2
    return index


def low_bit(k):
    return k & -k


def high_bit(k):
    return 1 << (k.bit_length() - 1)


def hop_of(k, piece):
    return high_bit(k) if piece == 0 else low_bit(k)


def layout_tables(levels, rows, cols):
    half_rows, half_cols = rows // 2, cols // 2
    per_level = rows * cols
    tokens = levels * per_level
    per_slot = tokens // SLOTS
    padded = -(-per_slot // 16) * 16
    gather = np.zeros((4 * per_level, 4 * per_level), np.float32)
    for i in range(2):
        for j in range(2):
            for a in range(rows):
                for b in range(cols):
                    out_row = (2 * i + j) * per_level + a * cols + b
                    gather[out_row, (2 * a + i) * 2 * cols + 2 * b + j] = 1
    to_slots = np.zeros((SLOTS * padded, tokens), np.float32)
    to_window = np.zeros((tokens, SLOTS * padded), np.float32)
    groups = levels // 2
    window = tokens // groups
    part = window // SLOTS
    per_quarter = half_rows * half_cols
    for q in range(SLOTS):
        row_half, col_half = ((1, 1), (1, 0), (0, 1), (0, 0))[q]
        for f in range(levels):
            level = (f + 1) % levels
            for a in range(half_rows):
                for b in range(half_cols):
                    place = q * padded + (f * half_rows + a) * half_cols + b
                    natural = level * per_level + (row_half * half_rows + a) * cols
                    natural += col_half * half_cols + b
                    to_slots[place, natural] = 1
                    target = (f // 2) * window + q * part + (f % 2) * per_quarter
                    to_window[target + a * half_cols + b, place] = 1
    t = np.arange(window)
    row_id = t // (window // 2)
    level_id = (t // per_quarter) % 2
    row_bias = np.where(row_id[:, None] == row_id[None, :], 0.0, BLOCKED)
    level_bias = np.where(level_id[:, None] == level_id[None, :], 0.0, BLOCKED)
    return (
        gather,
        to_slots,
        to_window,
        row_bias.astype(np.float32),
        level_bias.astype(np.float32),
        padded,
    )


def normalize(values, norm_gain, norm_bias):
    average = jnp.mean(values, axis=-1, keepdims=True)
    centered = values - average
    spread = jnp.mean(centered * centered, axis=-1, keepdims=True)
    return centered * lax.rsqrt(spread + EPSILON) * norm_gain + norm_bias


def dot(a, b):
    return jnp.dot(a, b, preferred_element_type=jnp.float32)


def body(
    dims,
    x_ref,
    mg_ref,
    mb_ref,
    cg_ref,
    cb_ref,
    gather_ref,
    slots_ref,
    slots_t_ref,
    window_ref,
    window_t_ref,
    row_bias_ref,
    level_bias_ref,
    wm_in,
    wq_in,
    wo_in,
    out_ref,
    wm,
    wq,
    wo,
    patches,
    patch_normed,
    coarse,
    own_slots,
    frame,
    framed,
    projected,
    context,
    back_slots,
    home,
    bias,
    own_sem,
    lat_send,
    lat_recv,
    z_send,
    z_recv,
    core_send,
    core_recv,
    halo_send,
    halo_recv,
    back_send,
    back_recv,
):
    lat_count, lon_count, padded, levels = dims
    lat, lon = lax.axis_index("lat"), lax.axis_index("lon")
    core = lon % 2
    z_side = (lon // 2) % 2
    sources, weights = (wm_in, wq_in, wo_in), (wm, wq, wo)
    bits = [1 << b for b in range(lat_count.bit_length() - 1)]
    others = sorted(range(1, lat_count), key=lambda k: (bin(k).count("1"), k))
    up, down = (lat + lat_count - 1) % lat_count, (lat + 1) % lat_count
    left, right = (lon + lon_count - 1) % lon_count, (lon + 1) % lon_count
    z_peer, core_peer = swapped(lon, 2), swapped(lon, 1)

    barrier = pltpu.get_barrier_semaphore()
    greeted = [(swapped(lat, b), lon) for b in bits]
    greeted += [(lat, z_peer), (lat, core_peer)]
    greeted += [(up, lon), (down, lon), (lat, left), (lat, right), (up, left), (down, right)]
    for to_lat, to_lon in greeted:
        pl.semaphore_signal(
            barrier, inc=1, device_id={"lat": to_lat, "lon": to_lon}, device_id_type=MESH
        )
    pl.semaphore_wait(barrier, len(greeted))

    def columns(w, core_side, third):
        wide = weights[w].shape[2] // PARTS
        return pl.ds(pl.multiple_of((core_side * 3 + third) * wide, 128), wide)

    def third_of(piece):
        return z_side if piece == 0 else 2

    def remote(src, dst, send, recv, to_lat, to_lon):
        return pltpu.make_async_remote_copy(
            src_ref=src,
            dst_ref=dst,
            send_sem=send,
            recv_sem=recv,
            device_id={"lat": to_lat, "lon": to_lon},
            device_id_type=MESH,
        )

    def lat_copy(w, k, piece):
        hop = hop_of(k, piece)
        origin = swapped(lat, k ^ hop)
        cols = columns(w, core, third_of(piece))
        dst = weights[w].at[origin, :, cols]
        src = sources[w].at[:, cols] if k == hop else dst
        return remote(
            src, dst, lat_send.at[w, k, piece], lat_recv.at[w, k, piece], swapped(lat, hop), lon
        )

    def z_copy(w, k):
        block = weights[w].at[swapped(lat, k), :, columns(w, core, z_side)]
        return remote(block, block, z_send.at[w, k], z_recv.at[w, k], lat, z_peer)

    def core_copy(w, k, place):
        third = (z_side, 2, 1 - z_side)[place]
        block = weights[w].at[swapped(lat, k), :, columns(w, core, third)]
        return remote(
            block, block, core_send.at[w, k, place], core_recv.at[w, k, place], lat, core_peer
        )

    def start_own(w):
        for piece in range(2):
            for b in bits:
                lat_copy(w, b, piece).start()

    def pump_lat(w):
        for piece in range(2):
            for k in others:
                lat_copy(w, k, piece).wait_recv()
                for further in others:
                    if further != k and further ^ hop_of(further, piece) == k:
                        lat_copy(w, further, piece).start()
                if piece == 0:
                    z_copy(w, k).start()
                core_copy(w, k, piece).start()

    def pump_z(w):
        for k in others:
            z_copy(w, k).wait_recv()
            core_copy(w, k, 2).start()

    def finish(w):
        for k in others:
            for place in range(3):
                core_copy(w, k, place).wait_recv()

    def own_copy(w):
        return pltpu.make_async_copy(sources[w], weights[w].at[lat], own_sem.at[w])

    start_own(0)
    for w in range(3):
        own_copy(w).start()

    per_level = patches.shape[0] // levels
    width = x_ref.shape[2]
    for level in range(levels):
        moved = dot(gather_ref[...], x_ref[level])
        for ij in range(4):
            patches[pl.ds(level * per_level, per_level), pl.ds(ij * width, width)] = moved[
                ij * per_level : (ij + 1) * per_level
            ]
    patch_normed[...] = normalize(patches[...], mg_ref[...], mb_ref[...]).astype(jnp.bfloat16)

    last = jnp.where(lat == lat_count - 1, 1.0, 0.0)
    bias[0] = row_bias_ref[...] * last
    bias[1] = jnp.minimum(row_bias_ref[...] * last, level_bias_ref[...])

    pump_lat(0)
    start_own(1)
    pump_z(0)
    for w in range(3):
        own_copy(w).wait()
    finish(0)

    def project(left_value, weight, store):
        count, rows, cols = weight.shape
        step = 256

        def one(i, carry):
            at = pl.ds(pl.multiple_of(i * step, step), step)
            store(at, dot(left_value, weight[:, :, at].reshape(count * rows, step)))
            return carry

        lax.fori_loop(0, cols // step, one, 0)

    def store_coarse(at, value):
        coarse[:, at] = value.astype(jnp.bfloat16)

    project(patch_normed[...], wm, store_coarse)

    normed = normalize(coarse[...].astype(jnp.float32), cg_ref[...], cb_ref[...])
    own_slots[...] = dot(slots_ref[...], normed.astype(jnp.bfloat16)).astype(jnp.bfloat16)

    def halo_copy(q):
        rows = pl.ds(q * padded, padded)
        to_lat, to_lon = ((lat, left), (up, lon), (up, left))[q - 1]
        return remote(
            own_slots.at[rows], frame.at[rows], halo_send.at[q], halo_recv.at[q], to_lat, to_lon
        )

    def back_copy(q):
        rows = pl.ds(q * padded, padded)
        to_lat, to_lon = ((lat, right), (down, lon), (down, right))[q - 1]
        return remote(
            back_slots.at[rows], home.at[rows], back_send.at[q], back_recv.at[q], to_lat, to_lon
        )

    for q in (3, 2, 1):
        halo_copy(q).start()
    frame[pl.ds(0, padded)] = own_slots[pl.ds(0, padded)]
    pump_lat(1)
    start_own(2)
    pump_z(1)
    for q in (1, 2, 3):
        halo_copy(q).wait_recv()
    framed[...] = dot(window_ref[...], frame[...]).astype(jnp.bfloat16)
    finish(1)

    def store_projected(at, value):
        projected[:, at] = value.astype(jnp.bfloat16)

    project(framed[...], wq, store_projected)
    pump_lat(2)
    pump_z(2)

    model = context.shape[1]
    depth = model // HEADS2
    packed = 128 // depth
    window = bias.shape[1]
    scale = depth ** (-0.5)
    lane = lax.broadcasted_iota(jnp.int32, (window, 128), 1)
    masks = [(lane >= h * depth) & (lane < (h + 1) * depth) for h in range(packed)]

    for g in range(levels // 2):
        rows = pl.ds(g * window, window)

        def one_group(i, carry):
            def lanes(which):
                return pl.ds(pl.multiple_of(which * model + i * 128, 128), 128)

            queries = projected[rows, lanes(0)].astype(jnp.float32)
            keys = projected[rows, lanes(1)]
            values = projected[rows, lanes(2)]
            result = jnp.zeros((window, 128), jnp.float32)
            for h in range(packed):
                one_head = jnp.where(masks[h], queries, 0.0).astype(jnp.bfloat16)
                scores = lax.dot_general(
                    one_head, keys, (((1,), (1,)), ((), ())), preferred_element_type=jnp.float32
                )
                scores = scores * scale + bias[g]
                peak = jnp.max(scores, axis=-1, keepdims=True)
                shares = jnp.exp(scores - peak)
                total = jnp.sum(shares, axis=-1, keepdims=True)
                mixed = dot((shares / total).astype(jnp.bfloat16), values)
                result = jnp.where(masks[h], mixed, result)
            context[rows, pl.ds(pl.multiple_of(i * 128, 128), 128)] = result.astype(jnp.bfloat16)
            return carry

        lax.fori_loop(0, model // 128, one_group, 0)

    back_slots[...] = dot(window_t_ref[...], context[...]).astype(jnp.bfloat16)
    for q in (3, 2, 1):
        back_copy(q).start()
    home[pl.ds(0, padded)] = back_slots[pl.ds(0, padded)]
    finish(2)
    for q in (1, 2, 3):
        back_copy(q).wait_recv()
    ordered = dot(slots_t_ref[...], home[...]).astype(jnp.bfloat16)

    def store_out(at, value):
        out_ref[:, at] = (coarse[:, at].astype(jnp.float32) + value).astype(jnp.bfloat16)

    project(ordered, wo, store_out)

    for w in range(3):
        for k in others:
            for piece in range(2):
                lat_copy(w, k, piece).wait_send()
            z_copy(w, k).wait_send()
            for place in range(3):
                core_copy(w, k, place).wait_send()
    for q in (1, 2, 3):
        halo_copy(q).wait_send()
        back_copy(q).wait_send()


def shards(
    fine_input,
    merge_gain,
    merge_bias,
    merge_weight,
    coarse_gain,
    coarse_bias,
    coarse_qkv,
    coarse_out,
):
    lat_count, lon_count = lax.axis_size("lat"), lax.axis_size("lon")
    levels, fine_rows, fine_cols, width = fine_input.shape
    rows, cols = fine_rows // 2, fine_cols // 2
    model = merge_weight.shape[1]
    assert rows == 6 and cols == 12 and levels == 4
    assert lat_count & (lat_count - 1) == 0 and lon_count % 4 == 0
    gather, to_slots, to_window, row_bias, level_bias, padded = layout_tables(levels, rows, cols)
    tokens = levels * rows * cols
    half = jnp.bfloat16
    operands = (
        fine_input.reshape(levels, fine_rows * fine_cols, width),
        merge_gain.reshape(1, -1),
        merge_bias.reshape(1, -1),
        coarse_gain.reshape(1, -1),
        coarse_bias.reshape(1, -1),
        jnp.asarray(gather, half),
        jnp.asarray(to_slots, half),
        jnp.asarray(to_slots.T, half),
        jnp.asarray(to_window, half),
        jnp.asarray(to_window.T, half),
        jnp.asarray(row_bias),
        jnp.asarray(level_bias),
        merge_weight,
        coarse_qkv,
        coarse_out,
    )
    slots = SLOTS * padded
    window = tokens // (levels // 2)
    result = pl.pallas_call(
        functools.partial(body, (lat_count, lon_count, padded, levels)),
        out_shape=jax.ShapeDtypeStruct((tokens, model), half),
        in_specs=[pl.BlockSpec(memory_space=pltpu.VMEM)] * 12
        + [pl.BlockSpec(memory_space=pl.ANY)] * 3,
        out_specs=pl.BlockSpec(memory_space=pltpu.VMEM),
        scratch_shapes=[
            pltpu.VMEM((lat_count,) + merge_weight.shape, half),
            pltpu.VMEM((lat_count,) + coarse_qkv.shape, half),
            pltpu.VMEM((lat_count,) + coarse_out.shape, half),
            pltpu.VMEM((tokens, 4 * width), jnp.float32),
            pltpu.VMEM((tokens, 4 * width), half),
            pltpu.VMEM((tokens, model), half),
            pltpu.VMEM((slots, model), half),
            pltpu.VMEM((slots, model), half),
            pltpu.VMEM((tokens, model), half),
            pltpu.VMEM((tokens, 3 * model), half),
            pltpu.VMEM((tokens, model), half),
            pltpu.VMEM((slots, model), half),
            pltpu.VMEM((slots, model), half),
            pltpu.VMEM((2, window, window), jnp.float32),
            pltpu.SemaphoreType.DMA((3,)),
            pltpu.SemaphoreType.DMA((3, lat_count, 2)),
            pltpu.SemaphoreType.DMA((3, lat_count, 2)),
            pltpu.SemaphoreType.DMA((3, lat_count)),
            pltpu.SemaphoreType.DMA((3, lat_count)),
            pltpu.SemaphoreType.DMA((3, lat_count, 3)),
            pltpu.SemaphoreType.DMA((3, lat_count, 3)),
            pltpu.SemaphoreType.DMA((SLOTS,)),
            pltpu.SemaphoreType.DMA((SLOTS,)),
            pltpu.SemaphoreType.DMA((SLOTS,)),
            pltpu.SemaphoreType.DMA((SLOTS,)),
        ],
        compiler_params=pltpu.CompilerParams(collective_id=0, has_side_effects=True),
    )(*operands)
    return result.reshape(levels, rows, cols, model)


def solution(mesh):
    in_specs = (
        P(None, "lat", "lon", None),
        P(),
        P(),
        P("lat", None),
        P(),
        P(),
        P("lat", None),
        P("lat", None),
    )
    out_specs = P(None, "lat", "lon", None)
    return jax.shard_map(shards, mesh=mesh, in_specs=in_specs, out_specs=out_specs, check_vma=False)
```

time: 152 us -> 77.7 us (0.51)
  waiting for transfers between devices: 92.5 us -> 0 us
  Pallas kernels: 0 us -> 72 us
  matrix products: 17.1 us -> 0 us
  between operations: 13.3 us -> 0.02 us
  local copies, waits for them, and re-layouts: 17.8 us -> 5.42 us
  other arithmetic: 7.01 us -> 0 us
  starting transfers between devices: 3.1 us -> 0 us
    pallas_call x0 -> x1, Pallas kernels: none -> 72 us  [shards(): pl.pallas_call(functools.partial(body, (lat_count, lon_count, padded, lev...]
    all_gather x3 -> x0, waiting for transfers between devices: 62.8 us -> none  [fetch_weight(): return lax.all_gather(raw_weights[position], 'lat', axis=0, tiled=True)]
    ppermute x4 -> x0, waiting for transfers between devices: 27.6 us -> none  [passed_along(): return lax.ppermute(value, axis, pairs)]
    dot_general x8 -> x0, matrix products: 17.1 us -> none  [the longest x2 5.39 us: attend(): jnp.dot(flat_rows, qkv_weight, preferred_element_type=jnp.float32)]
    convert_element_type x9 -> x0, local copies, waits for them, and re-layouts: 9.1 us -> none  [the longest x3 4.11 us: merge_patches(): patches.astype(jnp.float32)]
    reshape x2 -> x6, local copies, waits for them, and re-layouts: 0.11 us -> 5.31 us  [the longest x2 2.22 us: shards(): return result.reshape(levels, rows, cols, model)]
    ppermute x4 -> x0, starting transfers between devices: 3.02 us -> none  [passed_along(): return lax.ppermute(value, axis, pairs)]
    reduce_sum x3 -> x0, other arithmetic: 2.72 us -> none  [the longest x2 2.01 us: normalize(): spread = jnp.mean(centered * centered, axis=-1, keepdims=True)]
  transfers between devices with their start and end apart: 7 -> 0, of which waited for: 6 -> 0; matrix products, arithmetic and copies ran while one was open for 24% -> 0% of each run, Pallas kernels for 0% -> 0%
where the time goes in v1:
time: 77.7 us; the launch traced here: 77.5 us
  Pallas kernels  72 us (93%)
  local copies, waits for them, and re-layouts  5.42 us (7%)
    pallas_call x1, Pallas kernels, shards(): pl.pallas_call(functools.partial(body, (lat_count, lon_count, padded, lev...  72 us
    reshape x2, local copies, waits for them, and re-layouts, shards(): return result.reshape(levels, rows, cols, model)  2.22 us

profile of v1, /device:TPU:0, one launch (start us, length us, event | category | flops | bytes accessed | tf_op | source)
XLA Modules:
  0.0 77.5 jit_solution(1636621186726141511)
XLA Ops:
  0.0 0.0 copy-start.2
  0.0 0.0 copy-start
  0.0 1.3 %reshape.21.cg_ref = f32[1,768]{1,0:T(1,128)} reshape(f32[768]{0:T(1024)} %param.19) | data formatting | bytes 6144 | tf_op jit(solution)/shard_map/reshape | solution.py:389
  1.3 0.0 copy-done.2
  1.3 0.6 reshape.22.cb_ref
  1.9 0.0 copy-done
  1.9 0.0 copy-start.1
  1.9 0.6 reshape.19.mg_ref
  2.5 0.1 copy-done.1
  2.6 0.6 reshape.20.mb_ref
  3.2 72.0 %shard_map.145 = bf16[288,768]{1,0:T(8,128)(2,1)} custom-call(bf16[4,288,384]{2,1,0:T(8,128)(2,1)} %bitcast.1, f32[1,1536]{1,0:T(1,128)} %reshape.19.mg_ref, f32[1,1536]{1,0:T(1,128)} %reshape.20.mb_ref, f32[1,768]{1,0:T(1,128)} %reshape.21.cg_ref, f32[1,768]{1,0:T(1,128)} %reshape.22.cb_ref, bf16[288,288]{1,0:T(8,128)(2,1)} %constant.14.clone.gather_ref, ...), custom_call_target="tpu_custom_call" | custom-call | tf_op jit(solution)/shard_map/pallas_call | solution.py:404
  75.3 1.1 %reshape.23 = bf16[4,6,12,768]{3,2,1,0:T(8,128)(2,1)S(1)} reshape(bf16[288,768]{1,0:T(8,128)(2,1)} %shard_map.145) | data formatting | bytes 884736 | tf_op jit(solution)/shard_map/reshape | solution.py:439
  76.4 1.1 %copy.17 = bf16[4,6,12,768]{3,0,2,1:T(4,128)(2,1)} copy(bf16[4,6,12,768]{3,2,1,0:T(8,128)(2,1)S(1)} %reshape.23) | data formatting | bytes 884736 | tf_op jit(solution)/shard_map/reshape | solution.py:439
Async XLA Ops:
  0.0 1.3 %copy-start.2 = (f32[768]{0:T(1024)S(1)}, f32[768]{0:T(1024)}, u32[]{:S(2)}) copy-start(f32[768]{0:T(1024)} %param.20) | copy-start | bytes 9220
  0.0 1.9 %copy-start = (f32[1536]{0:T(1024)S(1)}, f32[1536]{0:T(1024)}, u32[]{:S(2)}) copy-start(f32[1536]{0:T(1024)} %param.16) | copy-start | bytes 18436
  1.9 0.7 copy-start.1

commit v2 on v1

--- a/solution.py
+++ b/solution.py
@@ -63,9 +63,8 @@
             for a in range(half_rows):
                 for b in range(half_cols):
                     place = q * padded + (f * half_rows + a) * half_cols + b
-                    natural = level * per_level + (row_half * half_rows + a) * cols
-                    natural += col_half * half_cols + b
-                    to_slots[place, natural] = 1
+                    natural = (row_half * half_rows + a) * cols + col_half * half_cols + b
+                    to_slots[place, natural * levels + level] = 1
                     target = (f // 2) * window + q * part + (f % 2) * per_quarter
                     to_window[target + a * half_cols + b, place] = 1
     t = np.arange(window)
@@ -77,8 +76,8 @@
         gather,
         to_slots,
         to_window,
-        row_bias.astype(np.float32),
-        level_bias.astype(np.float32),
+        np.tile(row_bias, (1, 4)).astype(np.float32),
+        np.tile(level_bias, (1, 4)).astype(np.float32),
         padded,
     )
 
@@ -96,18 +95,18 @@
 
 def body(
     dims,
-    x_ref,
-    mg_ref,
-    mb_ref,
-    cg_ref,
-    cb_ref,
-    gather_ref,
-    slots_ref,
-    slots_t_ref,
-    window_ref,
-    window_t_ref,
-    row_bias_ref,
-    level_bias_ref,
+    x_in,
+    mg_in,
+    mb_in,
+    cg_in,
+    cb_in,
+    gather_in,
+    slots_in,
+    slots_t_in,
+    window_in,
+    window_t_in,
+    row_bias_in,
+    level_bias_in,
     wm_in,
     wq_in,
     wo_in,
@@ -137,6 +136,19 @@
     halo_recv,
     back_send,
     back_recv,
+    fetch_sem,
+    x_ref,
+    mg_ref,
+    mb_ref,
+    cg_ref,
+    cb_ref,
+    gather_ref,
+    slots_ref,
+    slots_t_ref,
+    window_ref,
+    window_t_ref,
+    row_bias_ref,
+    level_bias_ref,
 ):
     lat_count, lon_count, padded, levels = dims
     lat, lon = lax.axis_index("lat"), lax.axis_index("lon")
@@ -157,11 +169,44 @@
         pl.semaphore_signal(
             barrier, inc=1, device_id={"lat": to_lat, "lon": to_lon}, device_id_type=MESH
         )
+    outside = (
+        x_in,
+        mg_in,
+        mb_in,
+        cg_in,
+        cb_in,
+        gather_in,
+        slots_in,
+        slots_t_in,
+        window_in,
+        window_t_in,
+        row_bias_in,
+        level_bias_in,
+    )
+    inside = (
+        x_ref,
+        mg_ref,
+        mb_ref,
+        cg_ref,
+        cb_ref,
+        gather_ref,
+        slots_ref,
+        slots_t_ref,
+        window_ref,
+        window_t_ref,
+        row_bias_ref,
+        level_bias_ref,
+    )
+    fetches = [
+        pltpu.make_async_copy(outside[i], inside[i], fetch_sem.at[i]) for i in range(len(inside))
+    ]
+    for i in (0, 5, 1, 2, 3, 4, 6, 8, 10, 11, 7, 9):
+        fetches[i].start()
     pl.semaphore_wait(barrier, len(greeted))
 
-    def columns(w, core_side, third):
-        wide = weights[w].shape[2] // PARTS
-        return pl.ds(pl.multiple_of((core_side * 3 + third) * wide, 128), wide)
+    def part_rows(w, core_side, third):
+        tall = weights[w].shape[1] // PARTS
+        return pl.ds(pl.multiple_of((core_side * 3 + third) * tall, tall), tall)
 
     def third_of(piece):
         return z_side if piece == 0 else 2
@@ -179,39 +224,43 @@
     def lat_copy(w, k, piece):
         hop = hop_of(k, piece)
         origin = swapped(lat, k ^ hop)
-        cols = columns(w, core, third_of(piece))
-        dst = weights[w].at[origin, :, cols]
-        src = sources[w].at[:, cols] if k == hop else dst
+        rows = part_rows(w, core, third_of(piece))
+        dst = weights[w].at[origin, rows]
+        src = sources[w].at[rows] if k == hop else dst
         return remote(
             src, dst, lat_send.at[w, k, piece], lat_recv.at[w, k, piece], swapped(lat, hop), lon
         )
 
     def z_copy(w, k):
-        block = weights[w].at[swapped(lat, k), :, columns(w, core, z_side)]
+        block = weights[w].at[swapped(lat, k), part_rows(w, core, z_side)]
         return remote(block, block, z_send.at[w, k], z_recv.at[w, k], lat, z_peer)
 
     def core_copy(w, k, place):
         third = (z_side, 2, 1 - z_side)[place]
-        block = weights[w].at[swapped(lat, k), :, columns(w, core, third)]
+        block = weights[w].at[swapped(lat, k), part_rows(w, core, third)]
         return remote(
             block, block, core_send.at[w, k, place], core_recv.at[w, k, place], lat, core_peer
         )
 
     def start_own(w):
-        for piece in range(2):
-            for b in bits:
-                lat_copy(w, b, piece).start()
-
-    def pump_lat(w):
-        for piece in range(2):
-            for k in others:
-                lat_copy(w, k, piece).wait_recv()
-                for further in others:
-                    if further != k and further ^ hop_of(further, piece) == k:
-                        lat_copy(w, further, piece).start()
-                if piece == 0:
-                    z_copy(w, k).start()
-                core_copy(w, k, piece).start()
+        for step in range(2):
+            for at, b in enumerate(bits):
+                lat_copy(w, b, (step + at) % 2).start()
+
+    arrivals = [(k, piece) for k in others for piece in range(2)]
+    arrivals.sort(key=lambda a: (bin(a[0]).count("1"), (bits.index(hop_of(*a)) + a[1]) % 2))
+    firsts = [a for a in arrivals if a[0] in bits]
+    rest = [a for a in arrivals if a[0] not in bits]
+
+    def pump(w, which):
+        for k, piece in which:
+            lat_copy(w, k, piece).wait_recv()
+            for further in others:
+                if further != k and further ^ hop_of(further, piece) == k:
+                    lat_copy(w, further, piece).start()
+            if piece == 0:
+                z_copy(w, k).start()
+            core_copy(w, k, piece).start()
 
     def pump_z(w):
         for k in others:
@@ -230,22 +279,31 @@
     for w in range(3):
         own_copy(w).start()
 
-    per_level = patches.shape[0] // levels
+    per_level = patches.shape[1] // levels
     width = x_ref.shape[2]
+    fetches[0].wait()
+    fetches[5].wait()
     for level in range(levels):
         moved = dot(gather_ref[...], x_ref[level])
         for ij in range(4):
-            patches[pl.ds(level * per_level, per_level), pl.ds(ij * width, width)] = moved[
-                ij * per_level : (ij + 1) * per_level
-            ]
-    patch_normed[...] = normalize(patches[...], mg_ref[...], mb_ref[...]).astype(jnp.bfloat16)
-
+            for at in range(0, width, 128):
+                patches[
+                    (ij * width + at) // 128, pl.ds(level, per_level, stride=levels), :
+                ] = moved[ij * per_level : (ij + 1) * per_level, at : at + 128]
+    pump(0, firsts)
+    start_own(1)
+    fetches[1].wait()
+    fetches[2].wait()
+    whole = jnp.concatenate([patches[b] for b in range(patches.shape[0])], axis=1)
+    patch_normed[...] = normalize(whole, mg_ref[...][None], mb_ref[...][None]).astype(
+        jnp.bfloat16
+    )
+    pump(0, rest)
+    for i in (3, 4, 6, 7, 8, 9, 10, 11):
+        fetches[i].wait()
     last = jnp.where(lat == lat_count - 1, 1.0, 0.0)
     bias[0] = row_bias_ref[...] * last
     bias[1] = jnp.minimum(row_bias_ref[...] * last, level_bias_ref[...])
-
-    pump_lat(0)
-    start_own(1)
     pump_z(0)
     for w in range(3):
         own_copy(w).wait()
@@ -267,8 +325,12 @@
 
     project(patch_normed[...], wm, store_coarse)
 
-    normed = normalize(coarse[...].astype(jnp.float32), cg_ref[...], cb_ref[...])
+    pump(1, firsts)
+    normed = normalize(coarse[...].astype(jnp.float32), cg_ref[...][None], cb_ref[...][None])
     own_slots[...] = dot(slots_ref[...], normed.astype(jnp.bfloat16)).astype(jnp.bfloat16)
+
+    model = context.shape[1]
+    split = model // 2
 
     def halo_copy(q):
         rows = pl.ds(q * padded, padded)
@@ -277,18 +339,23 @@
             own_slots.at[rows], frame.at[rows], halo_send.at[q], halo_recv.at[q], to_lat, to_lon
         )
 
-    def back_copy(q):
-        rows = pl.ds(q * padded, padded)
+    def back_copy(q, half):
+        rows, lanes = pl.ds(q * padded, padded), pl.ds(half * split, split)
         to_lat, to_lon = ((lat, right), (down, lon), (down, right))[q - 1]
         return remote(
-            back_slots.at[rows], home.at[rows], back_send.at[q], back_recv.at[q], to_lat, to_lon
+            back_slots.at[rows, lanes],
+            home.at[rows, lanes],
+            back_send.at[q, half],
+            back_recv.at[q, half],
+            to_lat,
+            to_lon,
         )
 
     for q in (3, 2, 1):
         halo_copy(q).start()
     frame[pl.ds(0, padded)] = own_slots[pl.ds(0, padded)]
-    pump_lat(1)
     start_own(2)
+    pump(1, rest)
     pump_z(1)
     for q in (1, 2, 3):
         halo_copy(q).wait_recv()
@@ -299,10 +366,8 @@
         projected[:, at] = value.astype(jnp.bfloat16)
 
     project(framed[...], wq, store_projected)
-    pump_lat(2)
-    pump_z(2)
-
-    model = context.shape[1]
+    pump(2, firsts)
+
     depth = model // HEADS2
     packed = 128 // depth
     window = bias.shape[1]
@@ -310,40 +375,50 @@
     lane = lax.broadcasted_iota(jnp.int32, (window, 128), 1)
     masks = [(lane >= h * depth) & (lane < (h + 1) * depth) for h in range(packed)]
 
-    for g in range(levels // 2):
-        rows = pl.ds(g * window, window)
-
-        def one_group(i, carry):
-            def lanes(which):
-                return pl.ds(pl.multiple_of(which * model + i * 128, 128), 128)
-
-            queries = projected[rows, lanes(0)].astype(jnp.float32)
-            keys = projected[rows, lanes(1)]
-            values = projected[rows, lanes(2)]
-            result = jnp.zeros((window, 128), jnp.float32)
-            for h in range(packed):
-                one_head = jnp.where(masks[h], queries, 0.0).astype(jnp.bfloat16)
+    for half in range(2):
+        for g in range(levels // 2):
+            rows = pl.ds(g * window, window)
+
+            def one_group(i, carry):
+                def lanes(which):
+                    return pl.ds(pl.multiple_of(which * model + i * 128, 128), 128)
+
+                queries = projected[rows, lanes(0)]
+                keys = projected[rows, lanes(1)]
+                values = projected[rows, lanes(2)]
+                nothing = jnp.zeros_like(queries)
+                stacked = jnp.concatenate([jnp.where(m, queries, nothing) for m in masks], axis=0)
                 scores = lax.dot_general(
-                    one_head, keys, (((1,), (1,)), ((), ())), preferred_element_type=jnp.float32
+                    keys, stacked, (((1,), (1,)), ((), ())), preferred_element_type=jnp.float32
                 )
                 scores = scores * scale + bias[g]
-                peak = jnp.max(scores, axis=-1, keepdims=True)
+                peak = jnp.max(scores, axis=0, keepdims=True)
                 shares = jnp.exp(scores - peak)
-                total = jnp.sum(shares, axis=-1, keepdims=True)
-                mixed = dot((shares / total).astype(jnp.bfloat16), values)
-                result = jnp.where(masks[h], mixed, result)
-            context[rows, pl.ds(pl.multiple_of(i * 128, 128), 128)] = result.astype(jnp.bfloat16)
-            return carry
-
-        lax.fori_loop(0, model // 128, one_group, 0)
-
-    back_slots[...] = dot(window_t_ref[...], context[...]).astype(jnp.bfloat16)
-    for q in (3, 2, 1):
-        back_copy(q).start()
-    home[pl.ds(0, padded)] = back_slots[pl.ds(0, padded)]
+                total = jnp.sum(shares, axis=0, keepdims=True)
+                probs = (shares * (1.0 / total)).astype(jnp.bfloat16)
+                mixed = lax.dot_general(
+                    probs, values, (((0,), (0,)), ((), ())), preferred_element_type=jnp.float32
+                )
+                result = mixed[:window]
+                for h in range(1, packed):
+                    result = jnp.where(masks[h], mixed[h * window : (h + 1) * window], result)
+                at = pl.ds(pl.multiple_of(i * 128, 128), 128)
+                context[rows, at] = result.astype(jnp.bfloat16)
+                return carry
+
+            lax.fori_loop(half * split // 128, (half + 1) * split // 128, one_group, 0)
+        lanes_of = pl.ds(half * split, split)
+        back_slots[:, lanes_of] = dot(window_t_ref[...], context[:, lanes_of]).astype(jnp.bfloat16)
+        for q in (3, 2, 1):
+            back_copy(q, half).start()
+        home[pl.ds(0, padded), lanes_of] = back_slots[pl.ds(0, padded), lanes_of]
+        if half == 0:
+            pump(2, rest)
+            pump_z(2)
     finish(2)
     for q in (1, 2, 3):
-        back_copy(q).wait_recv()
+        for half in range(2):
+            back_copy(q, half).wait_recv()
     ordered = dot(slots_t_ref[...], home[...]).astype(jnp.bfloat16)
 
     def store_out(at, value):
@@ -360,7 +435,8 @@
                 core_copy(w, k, place).wait_send()
     for q in (1, 2, 3):
         halo_copy(q).wait_send()
-        back_copy(q).wait_send()
+        for half in range(2):
+            back_copy(q, half).wait_send()
 
 
 def shards(
@@ -384,10 +460,10 @@
     half = jnp.bfloat16
     operands = (
         fine_input.reshape(levels, fine_rows * fine_cols, width),
-        merge_gain.reshape(1, -1),
-        merge_bias.reshape(1, -1),
-        coarse_gain.reshape(1, -1),
-        coarse_bias.reshape(1, -1),
+        merge_gain,
+        merge_bias,
+        coarse_gain,
+        coarse_bias,
         jnp.asarray(gather, half),
         jnp.asarray(to_slots, half),
         jnp.asarray(to_slots.T, half),
@@ -404,14 +480,13 @@
     result = pl.pallas_call(
         functools.partial(body, (lat_count, lon_count, padded, levels)),
         out_shape=jax.ShapeDtypeStruct((tokens, model), half),
-        in_specs=[pl.BlockSpec(memory_space=pltpu.VMEM)] * 12
-        + [pl.BlockSpec(memory_space=pl.ANY)] * 3,
+        in_specs=[pl.BlockSpec(memory_space=pl.ANY)] * len(operands),
         out_specs=pl.BlockSpec(memory_space=pltpu.VMEM),
         scratch_shapes=[
             pltpu.VMEM((lat_count,) + merge_weight.shape, half),
             pltpu.VMEM((lat_count,) + coarse_qkv.shape, half),
             pltpu.VMEM((lat_count,) + coarse_out.shape, half),
-            pltpu.VMEM((tokens, 4 * width), jnp.float32),
+            pltpu.VMEM((4 * width // 128, tokens, 128), jnp.float32),
             pltpu.VMEM((tokens, 4 * width), half),
             pltpu.VMEM((tokens, model), half),
             pltpu.VMEM((slots, model), half),
@@ -421,7 +496,7 @@
             pltpu.VMEM((tokens, model), half),
             pltpu.VMEM((slots, model), half),
             pltpu.VMEM((slots, model), half),
-            pltpu.VMEM((2, window, window), jnp.float32),
+            pltpu.VMEM((2, window, 4 * window), jnp.float32),
             pltpu.SemaphoreType.DMA((3,)),
             pltpu.SemaphoreType.DMA((3, lat_count, 2)),
             pltpu.SemaphoreType.DMA((3, lat_count, 2)),
@@ -431,12 +506,14 @@
             pltpu.SemaphoreType.DMA((3, lat_count, 3)),
             pltpu.SemaphoreType.DMA((SLOTS,)),
             pltpu.SemaphoreType.DMA((SLOTS,)),
-            pltpu.SemaphoreType.DMA((SLOTS,)),
-            pltpu.SemaphoreType.DMA((SLOTS,)),
-        ],
+            pltpu.SemaphoreType.DMA((SLOTS, 2)),
+            pltpu.SemaphoreType.DMA((SLOTS, 2)),
+            pltpu.SemaphoreType.DMA((len(operands) - 3,)),
+        ]
+        + [pltpu.VMEM(operand.shape, operand.dtype) for operand in operands[:-3]],
         compiler_params=pltpu.CompilerParams(collective_id=0, has_side_effects=True),
     )(*operands)
-    return result.reshape(levels, rows, cols, model)
+    return result.reshape(rows, cols, levels, model).transpose(2, 0, 1, 3)
 
 
 def solution(mesh):

time: 77.7 us -> 60.2 us (0.77)
  Pallas kernels: 72 us -> 58.1 us
  local copies, waits for them, and re-layouts: 5.42 us -> 1.88 us
    pallas_call x1, Pallas kernels: 72 us -> 58.1 us  [shards(): pl.pallas_call(functools.partial(body, (lat_count, lon_count, padded, lev...]
    reshape x6 -> x1, local copies, waits for them, and re-layouts: 5.31 us -> 1.88 us  [shards(): return result.reshape(rows, cols, levels, model).transpose(2, 0, 1, 3)]
where the time goes in v2:
time: 60.2 us; the launch traced here: 60 us
  Pallas kernels  58.1 us (97%)
  local copies, waits for them, and re-layouts  1.88 us (3%)
    pallas_call x1, Pallas kernels, shards(): pl.pallas_call(functools.partial(body, (lat_count, lon_count, padded, lev...  58.1 us
    reshape x1, local copies, waits for them, and re-layouts, shards(): return result.reshape(rows, cols, levels, model).transpose(2, 0, 1, 3)  1.88 us

profile of v2, /device:TPU:0, one launch (start us, length us, event | category | flops | bytes accessed | tf_op | source)
XLA Modules:
  0.0 60.0 jit_solution(9843220790603147219)
XLA Ops:
  0.0 58.1 %shard_map.145 = bf16[288,768]{1,0:T(8,128)(2,1)} custom-call(bf16[4,288,384]{2,1,0:T(8,128)(2,1)} %bitcast.2, f32[1536]{0:T(1024)} %mg_in.1, f32[1536]{0:T(1024)} %mb_in.1, f32[768]{0:T(1024)} %cg_in.1, f32[768]{0:T(1024)} %cb_in.1, bf16[288,288]{1,0:T(8,128)(2,1)} %constant.14.clone.gather_in, bf16[320,288]{1,0:T(8,128)(2,1)} %constant.15.clone.slots_in, ...), custom_call_target="tpu_custom_call" | custom-call | tf_op jit(solution)/shard_map/pallas_call | solution.py:480
  58.2 1.9 %reshape.7 = bf16[6,12,4,768]{3,2,1,0:T(4,128)(2,1)} reshape(bf16[288,768]{1,0:T(8,128)(2,1)} %shard_map.145) | data formatting | bytes 884736 | tf_op jit(solution)/shard_map/reshape | solution.py:516

commit v3 on v2

--- a/solution.py
+++ b/solution.py
@@ -13,6 +13,7 @@
 MESH = pl.DeviceIdType.MESH
 BLOCKED = -1e30
 SLOTS = 4
+BACK_PARTS = 3
 PARTS = 6
 
 
@@ -305,6 +306,7 @@
     bias[0] = row_bias_ref[...] * last
     bias[1] = jnp.minimum(row_bias_ref[...] * last, level_bias_ref[...])
     pump_z(0)
+    start_own(2)
     for w in range(3):
         own_copy(w).wait()
     finish(0)
@@ -330,7 +332,7 @@
     own_slots[...] = dot(slots_ref[...], normed.astype(jnp.bfloat16)).astype(jnp.bfloat16)
 
     model = context.shape[1]
-    split = model // 2
+    split = model // BACK_PARTS
 
     def halo_copy(q):
         rows = pl.ds(q * padded, padded)
@@ -354,7 +356,6 @@
     for q in (3, 2, 1):
         halo_copy(q).start()
     frame[pl.ds(0, padded)] = own_slots[pl.ds(0, padded)]
-    start_own(2)
     pump(1, rest)
     pump_z(1)
     for q in (1, 2, 3):
@@ -375,7 +376,7 @@
     lane = lax.broadcasted_iota(jnp.int32, (window, 128), 1)
     masks = [(lane >= h * depth) & (lane < (h + 1) * depth) for h in range(packed)]
 
-    for half in range(2):
+    for half in range(BACK_PARTS):
         for g in range(levels // 2):
             rows = pl.ds(g * window, window)
 
@@ -417,7 +418,7 @@
             pump_z(2)
     finish(2)
     for q in (1, 2, 3):
-        for half in range(2):
+        for half in range(BACK_PARTS):
             back_copy(q, half).wait_recv()
     ordered = dot(slots_t_ref[...], home[...]).astype(jnp.bfloat16)
 
@@ -435,7 +436,7 @@
                 core_copy(w, k, place).wait_send()
     for q in (1, 2, 3):
         halo_copy(q).wait_send()
-        for half in range(2):
+        for half in range(BACK_PARTS):
             back_copy(q, half).wait_send()
 
 
@@ -506,8 +507,8 @@
             pltpu.SemaphoreType.DMA((3, lat_count, 3)),
             pltpu.SemaphoreType.DMA((SLOTS,)),
             pltpu.SemaphoreType.DMA((SLOTS,)),
-            pltpu.SemaphoreType.DMA((SLOTS, 2)),
-            pltpu.SemaphoreType.DMA((SLOTS, 2)),
+            pltpu.SemaphoreType.DMA((SLOTS, BACK_PARTS)),
+            pltpu.SemaphoreType.DMA((SLOTS, BACK_PARTS)),
             pltpu.SemaphoreType.DMA((len(operands) - 3,)),
         ]
         + [pltpu.VMEM(operand.shape, operand.dtype) for operand in operands[:-3]],

time: 60.2 us -> 59.8 us (level)
  no operation moved by 1% of the time
where the time goes in v3:
time: 59.8 us; the launch traced here: 59.6 us
  Pallas kernels  57.8 us (97%)
  local copies, waits for them, and re-layouts  1.88 us (3%)
    pallas_call x1, Pallas kernels, shards(): pl.pallas_call(functools.partial(body, (lat_count, lon_count, padded, lev...  57.8 us
    reshape x1, local copies, waits for them, and re-layouts, shards(): return result.reshape(rows, cols, levels, model).transpose(2, 0, 1, 3)  1.88 us

profile of v3, /device:TPU:0, one launch (start us, length us, event | category | flops | bytes accessed | tf_op | source)
XLA Modules:
  0.0 59.6 jit_solution(18202186746719278143)
XLA Ops:
  0.0 57.8 %shard_map.145 = bf16[288,768]{1,0:T(8,128)(2,1)} custom-call(bf16[4,288,384]{2,1,0:T(8,128)(2,1)} %bitcast.2, f32[1536]{0:T(1024)} %mg_in.1, f32[1536]{0:T(1024)} %mb_in.1, f32[768]{0:T(1024)} %cg_in.1, f32[768]{0:T(1024)} %cb_in.1, bf16[288,288]{1,0:T(8,128)(2,1)} %constant.14.clone.gather_in, bf16[320,288]{1,0:T(8,128)(2,1)} %constant.15.clone.slots_in, ...), custom_call_target="tpu_custom_call" | custom-call | tf_op jit(solution)/shard_map/pallas_call | solution.py:481
  57.8 1.9 %reshape.7 = bf16[6,12,4,768]{3,2,1,0:T(4,128)(2,1)} reshape(bf16[288,768]{1,0:T(8,128)(2,1)} %shard_map.145) | data formatting | bytes 884736 | tf_op jit(solution)/shard_map/reshape | solution.py:517

commit v4 on v3

--- a/solution.py
+++ b/solution.py
@@ -423,7 +423,8 @@
     ordered = dot(slots_t_ref[...], home[...]).astype(jnp.bfloat16)
 
     def store_out(at, value):
-        out_ref[:, at] = (coarse[:, at].astype(jnp.float32) + value).astype(jnp.bfloat16)
+        total = coarse[:, at].astype(jnp.float32) + value
+        out_ref[:, :, at] = total.reshape(-1, levels, total.shape[1]).astype(jnp.bfloat16)
 
     project(ordered, wo, store_out)
 
@@ -480,7 +481,7 @@
     window = tokens // (levels // 2)
     result = pl.pallas_call(
         functools.partial(body, (lat_count, lon_count, padded, levels)),
-        out_shape=jax.ShapeDtypeStruct((tokens, model), half),
+        out_shape=jax.ShapeDtypeStruct((rows * cols, levels, model), half),
         in_specs=[pl.BlockSpec(memory_space=pl.ANY)] * len(operands),
         out_specs=pl.BlockSpec(memory_space=pltpu.VMEM),
         scratch_shapes=[

time: 59.8 us -> 59.9 us (level)
    unnamed x0 -> x1, local copies, waits for them, and re-layouts: none -> 1.93 us
    reshape x1 -> x0, local copies, waits for them, and re-layouts: 1.88 us -> none  [shards(): return result.reshape(rows, cols, levels, model).transpose(2, 0, 1, 3)]
where the time goes in v4:
time: 59.9 us; the launch traced here: 59.7 us
  Pallas kernels  57.8 us (96%)
  local copies, waits for them, and re-layouts  1.93 us (3%)
    pallas_call x1, Pallas kernels, shards(): pl.pallas_call(functools.partial(body, (lat_count, lon_count, padded, lev...  57.8 us
    unnamed x1, local copies, waits for them, and re-layouts  1.93 us

profile of v4, /device:TPU:0, one launch (start us, length us, event | category | flops | bytes accessed | tf_op | source)
XLA Modules:
  0.0 59.7 jit_solution(11885263081615821099)
XLA Ops:
  0.0 57.8 %shard_map.145 = bf16[72,4,768]{2,1,0:T(4,128)(2,1)} custom-call(bf16[4,288,384]{2,1,0:T(8,128)(2,1)} %bitcast.5, f32[1536]{0:T(1024)} %mg_in.1, f32[1536]{0:T(1024)} %mb_in.1, f32[768]{0:T(1024)} %cg_in.1, f32[768]{0:T(1024)} %cb_in.1, bf16[288,288]{1,0:T(8,128)(2,1)} %constant.14.clone.gather_in, bf16[320,288]{1,0:T(8,128)(2,1)} %constant.15.clone.slots_in, ...), custom_call_target="tpu_custom_call" | custom-call | tf_op jit(solution)/shard_map/pallas_call | solution.py:482
  57.8 1.9 %copy.17 = bf16[4,6,12,768]{3,0,2,1:T(4,128)(2,1)} copy(bf16[4,6,12,768]{3,0,2,1:T(4,128)(2,1)} %bitcast.4) | data formatting | bytes 884736
